TPU v7x, 512 devices: a whole 4x4x16 slice. The times are simulated.
512 devices in a mesh: segment: 16 (over z), fsdp: 32 (over x, y, core).
Axes of the slice: x: 4, y: 4, z: 16, core: 2. Of those that a mesh axis runs over, the one named last changes fastest.
Arguments:
- activations: bfloat16 [16, 4096, 4096], P('segment', 'fsdp'), may hold values from -6 to 6
- output_grad: bfloat16 [16, 4096, 4096], P('segment', 'fsdp'), may hold values from -0.75 to 0.75
- blocks: bfloat16 [16, 96, 128, 128], P('segment', 'fsdp'), may hold values from -0.5 to 0.5
- block_ids: int32 [16, 96], P('segment', 'fsdp'), may hold values from 0 to 21503, as said below
- owner_counts: int32 [16, 32], P('segment', 'fsdp'), may hold values from 1 to 3, 60 in all within a row
Outputs:
- arriving: bfloat16 [16, 4096, 4096], P('segment', 'fsdp')
- block_grads: float32 [16, 96, 128, 128], P('segment', 'fsdp')
Inputs may be any that keep to these rules, and one draw needn't show every extreme that they name: `block_ids`: with ND = 32 and NF = 224, an id e names kind e // (NF ND), hidden block (e // ND) mod NF and width block e mod ND. The 96 ids of one layer, padding included, name exactly 32 distinct hidden blocks, and no hidden block is named by two ids of the same kind. An owner's live blocks are its first owner_counts slots; the counts of one layer sum to exactly 60.
All inputs are finite; a program needn't handle non-finite values.
Results may differ from a plain program's by a relative error of at most 0.018.
Values may be sent and summed in bfloat16 or wider, within the bound.
A program may use at most 128 MiB of HBM per device.

v0:
```python
import jax
import jax.numpy as jnp
from jax import lax
from jax.experimental import pallas as pl
from jax.experimental.pallas import tpu as pltpu
from jax.sharding import PartitionSpec as P

D = 4096
FF = 28672
BLK = 128
CAP = 3
ND = D // BLK
NF = FF // BLK
OWNERS = 32
SLOTS = OWNERS * CAP
PIECE = CAP * BLK
GRAIN = BLK // 2
PART = PIECE // GRAIN
HALF = PART // 2
TOK = 128
TRIPLES = 20
ENTRIES = 2 * TRIPLES
ZSENDS = 8
MESH = pl.DeviceIdType.MESH

ROW_SG, ROW_SU, ROW_SD, ROW_CG, ROW_CU, ROW_CD = range(6)
ROW_TERM, ROW_OUT, ROW_WGT, ROW_SUM = range(6, 10)


def write_tables(tile, table, keep):
    shape = (128, 128)
    lane = lax.broadcasted_iota(jnp.int32, shape, 1)
    sub = lax.broadcasted_iota(jnp.int32, shape, 0)

    def across(row):
        return jnp.broadcast_to(row, shape)

    def down(row):
        return across(row).T

    def total(mask, values):
        return jnp.sum(jnp.where(mask, values, 0), axis=0, keepdims=True)

    def put(row, values):
        table[row : row + 1, :] = values

    kind, hidden, width, live = (tile[r : r + 1, :] for r in range(4))
    valid = lane[0:1] < SLOTS
    hidden = jnp.where(valid, hidden, 1000)
    thrice = total(down(hidden) < across(hidden), 1)
    key = down(jnp.where(valid, kind * SLOTS + thrice, -1))
    width_down, live_down = down(width), down(live)
    slots, widths, full = [], [], None
    for k in range(3):
        match = (key == k * SLOTS + 3 * lane) & (lane < ND)
        slots.append(down(total(match, sub)))
        widths.append(down(total(match, width_down)))
        alive = total(match, live_down)
        full = alive if full is None else full * alive
    full = down(full)
    place = down(total(sub < lane, full))
    whole = full == 1
    pick = whole & (place == lane)
    for k in range(3):
        put(ROW_SG + k, 2 * (SLOTS + total(pick, slots[k] - SLOTS)))
        put(ROW_CG + k, total(pick, widths[k]))
    hit = whole & (3 * sub == across(thrice)) & (sub < ND)
    none = 3 * TRIPLES
    put(ROW_TERM, 2 * (none + total(hit, 3 * place + across(kind) - none)))
    late = whole & (place + TRIPLES == lane)
    entry_width = 64 + total(pick, widths[0] - 64) + total(late, widths[1] - 64)
    entry_slot = SLOTS + total(pick, slots[0] - SLOTS) + total(late, slots[1] - SLOTS)
    order = entry_width * 128 + lane[0:1]
    rank = down(total(down(order) < across(order), 1))
    entry_width = down(entry_width)
    chosen = rank == lane
    put(ROW_OUT, total(chosen, sub))
    put(ROW_WGT, 2 * total(chosen, down(entry_slot)))
    same = total(chosen, entry_width) == total(rank + 1 == lane, entry_width)
    same = down(jnp.where(same & (lane[0:1] > 0), 1, 0)).astype(jnp.float32)
    for m in range(ENTRIES):
        keep[m] = jnp.broadcast_to(same[m : m + 1, :], (8, 128))
    present = total(entry_width == lane, 1) > 0
    put(ROW_SUM, jnp.where(present, total(entry_width <= lane, 1), 0))


def kernel(
    ids,
    count,
    x_hbm,
    y_hbm,
    blocks_hbm,
    arriving,
    grads,
    x_flat,
    y_flat,
    x,
    y,
    wgt,
    meta_a,
    meta_b,
    meta_c,
    table,
    tbl,
    keep,
    hid,
    out_grad,
    sums,
    passed,
    zeros,
    terms,
    sib_out,
    sib_in,
    pair_two,
    one_in,
    pair_side,
    side_in,
    quad,
    far_in,
    near_in,
    local_sem,
    send_sem,
    recv_sem,
):
    z, f = lax.axis_index("segment"), lax.axis_index("fsdp")
    layers = lax.axis_size("segment")
    core = lax.rem(f, 2)
    yy, xx = lax.rem(lax.div(f, 2), 4), lax.div(f, 8)
    a = xx * (1 - core) + yy * core
    b = xx * core + yy * (1 - core)

    def owner(da, db):
        return lax.rem(a + da, 4) * (8 - 6 * core) + lax.rem(b + db, 4) * (2 + 6 * core) + core

    def sib_owner(da, db):
        return lax.rem(b + da, 4) * (2 + 6 * core) + lax.rem(a + db, 4) * (8 - 6 * core) + 1 - core

    sibling = f + 1 - 2 * core
    used = [0]

    def remote(src, dst, target):
        i = used[0]
        used[0] = i + 1
        return pltpu.make_async_remote_copy(
            src_ref=src,
            dst_ref=dst,
            send_sem=send_sem.at[i],
            recv_sem=recv_sem.at[i],
            device_id=target,
            device_id_type=MESH,
        )

    own_in = pltpu.make_async_copy(
        blocks_hbm, wgt.at[pl.ds(f * PART, PART)], local_sem.at[0]
    )
    x_in = pltpu.make_async_copy(x_hbm, x_flat, local_sem.at[1])
    y_in = pltpu.make_async_copy(y_hbm, y_flat, local_sem.at[2])
    own_in.start()
    x_in.start()
    y_in.start()

    barrier = pltpu.get_barrier_semaphore()
    partners = [{"fsdp": owner(d, 0)} for d in (1, 2, 3)]
    partners += [{"fsdp": owner(0, d)} for d in (1, 2, 3)]
    partners += [{"fsdp": sibling}]
    partners += [{"segment": lax.rem(z + d, layers)} for d in (1, layers - 1)]
    for partner in partners:
        pl.semaphore_signal(barrier, inc=1, device_id=partner, device_id_type=MESH)

    lane = lax.broadcasted_iota(jnp.int32, (8, 128), 1)
    sub = lax.broadcasted_iota(jnp.int32, (8, 128), 0)
    tile = jnp.zeros((8, 128), jnp.int32)
    alive = jnp.full((8, 128), count[0, 0], jnp.int32)
    for s in range(CAP):
        slot_id = jnp.full((8, 128), ids[0, s], jnp.int32)
        kind = jnp.where(slot_id >= NF * ND, 1, 0) + jnp.where(slot_id >= 2 * NF * ND, 1, 0)
        hidden = (slot_id - kind * (NF * ND)) >> 5
        width = slot_id & (ND - 1)
        live = jnp.where(alive > s, 1, 0)
        column = jnp.where(sub == 0, kind, jnp.where(sub == 1, hidden, jnp.where(sub == 2, width, live)))
        tile = tile + jnp.where((lane == CAP * f + s) & (sub < 4), column, 0)
    meta_a[0] = tile
    wgt[2 * SLOTS :] = jnp.zeros((2, GRAIN, BLK), jnp.bfloat16)
    terms[6 * TRIPLES :] = jnp.zeros((2, GRAIN, BLK), jnp.bfloat16)
    sums[0] = jnp.zeros((BLK, BLK), jnp.float32)

    own_in.wait()
    pl.semaphore_wait(barrier, len(partners))

    def piece(da, db, half=None):
        start = owner(da, db) * PART + (HALF if half == 1 else 0)
        return wgt.at[pl.ds(start, PART if half is None else HALF)]

    def forward(da, db, half, target):
        ref = piece(da, db, half)
        copy = remote(ref, ref, {"fsdp": target})
        copy.start()
        return copy

    sends = []

    def to_sibling(da, db):
        copy = forward(da, db, None, sibling)
        to_sib.append(copy)
        sends.append(copy)

    def push(da, db, half, target):
        copy = forward(da, db, half, target)
        sends.append(copy)
        return copy

    def spread(da):
        return push(da, 0, None, owner(0, 1)), push(da, 0, None, owner(0, 3))

    to_sib = []
    meta_one = [remote(meta_a.at[0], meta_a.at[d], {"fsdp": owner(d, 0)}) for d in (1, 2, 3)]
    for copy in meta_one:
        copy.start()
    right, left = push(0, 0, None, owner(1, 0)), push(0, 0, None, owner(3, 0))
    row_own = spread(0)
    to_sibling(0, 0)
    for copy in meta_one:
        copy.wait_recv()
    meta_b[0] = meta_a[0] + meta_a[1] + meta_a[2] + meta_a[3]
    meta_two = [remote(meta_b.at[0], meta_b.at[d], {"fsdp": owner(0, d)}) for d in (1, 2, 3)]
    for copy in meta_two:
        copy.start()
    right.wait_recv()
    far_right = push(3, 0, 0, owner(1, 0))
    row_left = spread(3)
    to_sibling(3, 0)
    left.wait_recv()
    far_left = push(1, 0, 1, owner(3, 0))
    row_right = spread(1)
    to_sibling(1, 0)
    for copy in meta_two:
        copy.wait_recv()
    meta_c[0] = meta_b[0] + meta_b[1] + meta_b[2] + meta_b[3]
    meta_three = remote(meta_c.at[0], meta_c.at[1], {"fsdp": sibling})
    meta_three.start()

    halves = []

    def pass_on(row, da):
        row[0].wait_recv()
        first = push(da, 3, 0, owner(0, 1))
        to_sibling(da, 3)
        row[1].wait_recv()
        second = push(da, 1, 1, owner(0, 3))
        to_sibling(da, 1)
        halves.append((da, first, second))

    def finish():
        da, first, second = halves.pop(0)
        first.wait_recv()
        second.wait_recv()
        to_sibling(da, 2)

    pass_on(row_own, 0)
    far_right.wait_recv()
    far_left.wait_recv()
    row_far = spread(2)
    to_sibling(2, 0)
    meta_three.wait_recv()
    write_tables(meta_c[0] + meta_c[1], table, keep)
    to_scalar = pltpu.make_async_copy(table, tbl, local_sem.at[3])
    to_scalar.start()
    x_in.wait()
    y_in.wait()
    for i in range(ND):
        x[i] = x_flat[:, i * BLK : (i + 1) * BLK]
        y[i] = y_flat[:, i * BLK : (i + 1) * BLK]
    pass_on(row_left, 3)
    pass_on(row_right, 1)
    finish()
    pass_on(row_far, 2)
    finish()
    finish()
    finish()
    to_scalar.wait()
    for copy in to_sib:
        copy.wait_recv()

    def at(row, k):
        return tbl[row, k]

    def weight(i):
        return wgt[pl.ds(i, 2)].reshape(BLK, BLK)

    def dot(left_side, right_side, dims):
        return lax.dot_general(left_side, right_side, (dims, ((), ())), preferred_element_type=jnp.float32)

    def products(step, carry):
        for inner in range(4):
            k = step * 4 + inner
            gate = dot(x[at(ROW_CG, k)], weight(at(ROW_SG, k)), ((1,), (0,)))
            up = dot(x[at(ROW_CU, k)], weight(at(ROW_SU, k)), ((1,), (0,)))
            back = dot(y[at(ROW_CD, k)], weight(at(ROW_SD, k)), ((1,), (1,)))
            sigmoid = jax.nn.sigmoid(gate)
            silu = gate * sigmoid
            hid[k] = (silu * up).astype(jnp.bfloat16)
            out_grad[k] = (back * up * sigmoid * (1.0 + gate * (1.0 - sigmoid))).astype(
                jnp.bfloat16
            )
            out_grad[k + TRIPLES] = (back * silu).astype(jnp.bfloat16)
        return carry

    lax.fori_loop(0, TRIPLES // 4, products, 0)

    def widths(step, carry):
        made = []
        for inner in range(4):
            m = step * 4 + inner
            made.append(
                dot(
                    out_grad[at(ROW_OUT, m)],
                    weight(at(ROW_WGT, m)),
                    ((1,), (1,)),
                )
            )
        for inner in range(4):
            m = step * 4 + inner
            run = made[inner] + sums[m] * keep[m, 0:1, :]
            sums[m + 1] = run
        return carry

    lax.fori_loop(0, ENTRIES // 4, widths, 0)

    wide = D // ZSENDS
    z_sends = []
    for j in range(ZSENDS):
        for i in range(j * ND // ZSENDS, (j + 1) * ND // ZSENDS):
            passed[:, i * BLK : (i + 1) * BLK] = (
                y[i].astype(jnp.float32) + sums[at(ROW_SUM, i)]
            ).astype(jnp.bfloat16)
        here = pl.ds(j * wide, wide)
        copy = remote(
            passed.at[:, here], arriving.at[:, here], {"segment": lax.rem(z + layers - 1, layers)}
        )
        z_sends.append(copy)

        @pl.when(z > 0)
        def _(copy=copy):
            copy.start()

    def slot_terms(step, carry):
        for inner in range(2):
            k = step * 2 + inner
            made = (
                dot(x[at(ROW_CG, k)], out_grad[k], ((0,), (0,))),
                dot(x[at(ROW_CU, k)], out_grad[k + TRIPLES], ((0,), (0,))),
                dot(hid[k], y[at(ROW_CD, k)], ((0,), (0,))),
            )
            for n in range(3):
                terms[pl.ds(6 * k + 2 * n, 2)] = made[n].astype(jnp.bfloat16).reshape(2, GRAIN, BLK)
        return carry

    lax.fori_loop(0, TRIPLES // 2, slot_terms, 0)

    group = 4 * PART

    def term(device, g):
        return terms[at(ROW_TERM, CAP * device + lax.div(g, 2)) + lax.rem(g, 2)]

    def each(low, high, step):
        def run(t, carry):
            step(t)
            return carry

        lax.fori_loop(low, high, run, 0)

    sib_copies = {}
    for db in (2, 1, 3, 0):

        def pack(t, db=db):
            sib_out[db, t] = term(sib_owner(lax.div(t, PART), db), lax.rem(t, PART))

        each(0, group, pack)
        copy = remote(sib_out.at[db], sib_in.at[db], {"fsdp": sibling})
        copy.start()
        sends.append(copy)
        sib_copies[db] = copy

    def paired(db, t):
        own = term(owner(lax.div(t, PART), db), lax.rem(t, PART))
        return own.astype(jnp.float32) + sib_in[db, t].astype(jnp.float32)

    def reduce_to(src, dst, target):
        copy = remote(src, dst, {"fsdp": target})
        copy.start()
        sends.append(copy)
        return copy

    sib_copies[2].wait_recv()

    def pair_far(t):
        pair_two[t] = paired(2, t).astype(jnp.bfloat16)

    each(0, group, pair_far)
    middle = group // 2
    up_one = reduce_to(pair_two.at[0:middle], one_in.at[0:middle], owner(0, 1))
    down_one = reduce_to(pair_two.at[middle:], one_in.at[middle:], owner(0, 3))
    side_copies = []
    for n, (db, came) in enumerate(((1, up_one), (3, down_one))):

        def with_far(t, n=n, db=db):
            pair_side[n, t] = (paired(db, t) + one_in[t].astype(jnp.float32)).astype(jnp.bfloat16)

        def alone(t, n=n, db=db):
            pair_side[n, t] = paired(db, t).astype(jnp.bfloat16)

        sib_copies[db].wait_recv()
        each(middle * (1 - n), middle * (2 - n), alone)
        came.wait_recv()
        each(middle * n, middle * (n + 1), with_far)
        side_copies.append(reduce_to(pair_side.at[n], side_in.at[n], owner(0, db)))
    sib_copies[0].wait_recv()
    for copy in side_copies:
        copy.wait_recv()

    def ringed(da, t):
        i = PART * da + t
        value = term(owner(da, 0), t).astype(jnp.float32) + sib_in[0, i].astype(jnp.float32)
        return value + side_in[0, i].astype(jnp.float32) + side_in[1, i].astype(jnp.float32)

    def opposite(t):
        quad[2, t] = ringed(2, t).astype(jnp.bfloat16)

    each(0, PART, opposite)
    up_far = reduce_to(quad.at[2, 0:HALF], far_in.at[0:HALF], owner(1, 0))
    down_far = reduce_to(quad.at[2, HALF:], far_in.at[HALF:], owner(3, 0))
    near_copies = []
    for n, (da, came) in enumerate(((1, up_far), (3, down_far))):

        def with_opposite(t, da=da):
            quad[da, t] = (ringed(da, t) + far_in[t].astype(jnp.float32)).astype(jnp.bfloat16)

        def only(t, da=da):
            quad[da, t] = ringed(da, t).astype(jnp.bfloat16)

        each(HALF * (1 - n), HALF * (2 - n), only)
        came.wait_recv()
        each(HALF * n, HALF * (n + 1), with_opposite)
        near_copies.append(reduce_to(quad.at[da], near_in.at[n], owner(da, 0)))
    for copy in near_copies:
        copy.wait_recv()

    def final(t):
        grads[t] = ringed(0, t) + near_in[0, t].astype(jnp.float32) + near_in[1, t].astype(jnp.float32)

    each(0, PART, final)

    @pl.when(z == layers - 1)
    def _():
        zeros[...] = jnp.zeros(zeros.shape, jnp.bfloat16)
        fill = pltpu.make_async_copy(zeros, arriving, local_sem.at[4])
        fill.start()
        fill.wait()

    for copy in meta_one + meta_two + [meta_three] + sends:
        copy.wait_send()
    for copy in z_sends:

        @pl.when(z < layers - 1)
        def _(copy=copy):
            copy.wait_recv()

        @pl.when(z > 0)
        def _(copy=copy):
            copy.wait_send()


COPIES = 7 + 4 + 16 + 16 + ZSENDS + 4 + 4 + 4


def body(activations, output_grad, blocks, block_ids, owner_counts):
    bf16, f32 = jnp.bfloat16, jnp.float32
    hbm = pl.BlockSpec(memory_space=pltpu.HBM)
    free = pl.BlockSpec(memory_space=pl.ANY)
    smem = pl.BlockSpec(memory_space=pltpu.SMEM)
    vmem = pl.BlockSpec(memory_space=pltpu.VMEM)
    arriving, grads = pl.pallas_call(
        kernel,
        out_shape=(
            jax.ShapeDtypeStruct((TOK, D), bf16),
            jax.ShapeDtypeStruct((PART, GRAIN, BLK), f32),
        ),
        in_specs=[smem, smem, hbm, hbm, hbm],
        out_specs=(free, vmem),
        scratch_shapes=[
            pltpu.VMEM((TOK, D), bf16),
            pltpu.VMEM((TOK, D), bf16),
            pltpu.VMEM((ND, TOK, BLK), bf16),
            pltpu.VMEM((ND, TOK, BLK), bf16),
            pltpu.VMEM((2 * SLOTS + 2, GRAIN, BLK), bf16),
            pltpu.VMEM((4, 8, 128), jnp.int32),
            pltpu.VMEM((4, 8, 128), jnp.int32),
            pltpu.VMEM((2, 8, 128), jnp.int32),
            pltpu.VMEM((16, 128), jnp.int32),
            pltpu.SMEM((16, 128), jnp.int32),
            pltpu.VMEM((ENTRIES, 8, 128), f32),
            pltpu.VMEM((TRIPLES, TOK, BLK), bf16),
            pltpu.VMEM((ENTRIES, TOK, BLK), bf16),
            pltpu.VMEM((ENTRIES + 1, TOK, BLK), f32),
            pltpu.VMEM((TOK, D), bf16),
            pltpu.VMEM((TOK, D), bf16),
            pltpu.VMEM((6 * TRIPLES + 2, GRAIN, BLK), bf16),
            pltpu.VMEM((4, 4 * PART, GRAIN, BLK), bf16),
            pltpu.VMEM((4, 4 * PART, GRAIN, BLK), bf16),
            pltpu.VMEM((4 * PART, GRAIN, BLK), bf16),
            pltpu.VMEM((4 * PART, GRAIN, BLK), bf16),
            pltpu.VMEM((2, 4 * PART, GRAIN, BLK), bf16),
            pltpu.VMEM((2, 4 * PART, GRAIN, BLK), bf16),
            pltpu.VMEM((4, PART, GRAIN, BLK), bf16),
            pltpu.VMEM((PART, GRAIN, BLK), bf16),
            pltpu.VMEM((2, PART, GRAIN, BLK), bf16),
            pltpu.SemaphoreType.DMA((5,)),
            pltpu.SemaphoreType.DMA((COPIES,)),
            pltpu.SemaphoreType.DMA((COPIES,)),
        ],
        compiler_params=pltpu.CompilerParams(
            collective_id=0, has_side_effects=True, vmem_limit_bytes=48 * 1024 * 1024
        ),
        name="relay",
    )(
        block_ids,
        owner_counts,
        activations.reshape(TOK, D),
        output_grad.reshape(TOK, D),
        blocks.reshape(PART, GRAIN, BLK),
    )
    return arriving.reshape(1, TOK, D), grads.reshape(1, CAP, BLK, BLK)


def solution(mesh):
    placed = (
        P("segment", "fsdp", None),
        P("segment", "fsdp", None),
        P("segment", "fsdp", None, None),
        P("segment", "fsdp"),
        P("segment", "fsdp"),
    )
    return jax.shard_map(
        body,
        mesh=mesh,
        in_specs=placed,
        out_specs=(P("segment", "fsdp", None), P("segment", "fsdp", None, None)),
        check_vma=False,
    )
```

profile of v0, /device:TPU:30, one launch (start us, length us, event | category | flops | bytes accessed | tf_op | source)
XLA Modules:
  0.0 67.4 jit_solution(18164758319113972695)
XLA Ops:
  1.3 0.0 copy-start.3
  1.3 0.6 copy-done.3
  1.9 0.0 copy-start
  1.9 1.2 %copy-done = bf16[1,128,4096]{2,1,0:T(8,128)(2,1)S(1)} copy-done((bf16[1,128,4096]{2,1,0:T(8,128)(2,1)S(1)}, bf16[1,128,4096]{2,1,0:T(8,128)(2,1)}, u32[]{:S(2)}) %copy-start) | copy-done | bytes 1048600
  3.2 0.0 copy-start.1
  3.2 1.2 %copy-done.1 = bf16[1,128,4096]{2,1,0:T(8,128)(2,1)S(1)} copy-done((bf16[1,128,4096]{2,1,0:T(8,128)(2,1)S(1)}, bf16[1,128,4096]{2,1,0:T(8,128)(2,1)}, u32[]{:S(2)}) %copy-start.1) | copy-done | bytes 1048600
  4.4 0.0 copy-start.2
  4.4 0.9 %copy-done.2 = bf16[1,3,128,128]{3,2,1,0:T(8,128)(2,1)S(1)} copy-done((bf16[1,3,128,128]{3,2,1,0:T(8,128)(2,1)S(1)}, bf16[1,3,128,128]{3,2,1,0:T(8,128)(2,1)}, u32[]{:S(2)}) %copy-start.2) | copy-done | bytes 98328
  5.3 60.4 %relay.1 = (bf16[128,4096]{1,0:T(8,128)(2,1)S(1)}, f32[6,64,128]{2,1,0:T(8,128)S(1)}) custom-call(s32[1,3]{1,0:T(1,128)S(1)} %copy-done.3, s32[1,1]{1,0:T(1,128)S(6)} %copy.9.count, bf16[128,4096]{1,0:T(8,128)(2,1)S(1)} %bitcast.5, bf16[128,4096]{1,0:T(8,128)(2,1)S(1)} %bitcast.6, bf16[6,64,128]{2,1,0:T(8,128)(2,1)S(1)} %bitcast.9), custom_call_target="tpu_custom_call" | custom-call | tf_op jit(solution)/shard_map/relay/pallas_call | solution.py:482
  65.7 1.0 %copy.10 = bf16[1,128,4096]{2,1,0:T(8,128)(2,1)} copy(bf16[1,128,4096]{2,1,0:T(8,128)(2,1)S(1)} %bitcast.7) | data formatting | bytes 2097152
  66.7 0.7 %copy.11 = f32[1,3,128,128]{3,2,1,0:T(8,128)} copy(f32[1,3,128,128]{3,2,1,0:T(8,128)S(1)} %bitcast.8) | data formatting | bytes 393216
Async XLA Ops:
  1.3 0.7 copy-start.3
  1.9 1.2 %copy-start = (bf16[1,128,4096]{2,1,0:T(8,128)(2,1)S(1)}, bf16[1,128,4096]{2,1,0:T(8,128)(2,1)}, u32[]{:S(2)}) copy-start(bf16[1,128,4096]{2,1,0:T(8,128)(2,1)} %param.5) | copy-start | bytes 3145732
  3.2 1.2 %copy-start.1 = (bf16[1,128,4096]{2,1,0:T(8,128)(2,1)S(1)}, bf16[1,128,4096]{2,1,0:T(8,128)(2,1)}, u32[]{:S(2)}) copy-start(bf16[1,128,4096]{2,1,0:T(8,128)(2,1)} %param.6) | copy-start | bytes 3145732
  4.4 0.9 %copy-start.2 = (bf16[1,3,128,128]{3,2,1,0:T(8,128)(2,1)S(1)}, bf16[1,3,128,128]{3,2,1,0:T(8,128)(2,1)}, u32[]{:S(2)}) copy-start(bf16[1,3,128,128]{3,2,1,0:T(8,128)(2,1)} %param.7) | copy-start | bytes 294916
where the time goes:
time: 67.6 us; the launch traced here: 67.4 us
  Pallas kernels  60.4 us (89%)
  local copies, waits for them, and re-layouts  5.64 us (8%)
  between operations  1.3 us (2%)
    pallas_call x1, Pallas kernels, body(): pl.pallas_call(kernel, out_shape=(jax.ShapeDtypeStruct((TOK, D), bf16), j...  60.4 us
    unnamed x10, local copies, waits for them, and re-layouts  5.64 us

commit v1 on v0

--- a/solution.py
+++ b/solution.py
@@ -24,7 +24,9 @@
 MESH = pl.DeviceIdType.MESH
 
 ROW_SG, ROW_SU, ROW_SD, ROW_CG, ROW_CU, ROW_CD = range(6)
-ROW_TERM, ROW_OUT, ROW_WGT, ROW_SUM = range(6, 10)
+ROW_LEFT, ROW_RIGHT, ROW_OUT, ROW_WGT, ROW_SUM = range(6, 11)
+AT_Y, AT_GATE, AT_UP, AT_ZERO = ND, 2 * ND, 2 * ND + TRIPLES, 2 * ND + ENTRIES
+AT_HID, AT_NONE = ND, ND + TRIPLES
 
 
 def write_tables(tile, table, keep):
@@ -63,10 +65,13 @@
     pick = whole & (place == lane)
     for k in range(3):
         put(ROW_SG + k, 2 * (SLOTS + total(pick, slots[k] - SLOTS)))
-        put(ROW_CG + k, total(pick, widths[k]))
+        put(ROW_CG + k, total(pick, widths[k]) + (AT_Y if k == 2 else 0))
     hit = whole & (3 * sub == across(thrice)) & (sub < ND)
-    none = 3 * TRIPLES
-    put(ROW_TERM, 2 * (none + total(hit, 3 * place + across(kind) - none)))
+    found, spot = total(hit, 1), total(hit, place)
+    left = jnp.where(kind == 2, AT_HID + spot, width)
+    right = jnp.where(kind == 2, AT_Y + width, AT_GATE + TRIPLES * kind + spot)
+    put(ROW_LEFT, AT_NONE + found * (left - AT_NONE))
+    put(ROW_RIGHT, AT_ZERO + found * (right - AT_ZERO))
     late = whole & (place + TRIPLES == lane)
     entry_width = 64 + total(pick, widths[0] - 64) + total(late, widths[1] - 64)
     entry_slot = SLOTS + total(pick, slots[0] - SLOTS) + total(late, slots[1] - SLOTS)
@@ -74,7 +79,7 @@
     rank = down(total(down(order) < across(order), 1))
     entry_width = down(entry_width)
     chosen = rank == lane
-    put(ROW_OUT, total(chosen, sub))
+    put(ROW_OUT, AT_GATE + total(chosen, sub))
     put(ROW_WGT, 2 * total(chosen, down(entry_slot)))
     same = total(chosen, entry_width) == total(rank + 1 == lane, entry_width)
     same = down(jnp.where(same & (lane[0:1] > 0), 1, 0)).astype(jnp.float32)
@@ -94,8 +99,8 @@
     grads,
     x_flat,
     y_flat,
-    x,
-    y,
+    plain,
+    turned,
     wgt,
     meta_a,
     meta_b,
@@ -103,20 +108,14 @@
     table,
     tbl,
     keep,
-    hid,
-    out_grad,
     sums,
     passed,
     zeros,
-    terms,
     sib_out,
     sib_in,
-    pair_two,
-    one_in,
-    pair_side,
+    pair_out,
     side_in,
     quad,
-    far_in,
     near_in,
     local_sem,
     send_sem,
@@ -181,7 +180,8 @@
         tile = tile + jnp.where((lane == CAP * f + s) & (sub < 4), column, 0)
     meta_a[0] = tile
     wgt[2 * SLOTS :] = jnp.zeros((2, GRAIN, BLK), jnp.bfloat16)
-    terms[6 * TRIPLES :] = jnp.zeros((2, GRAIN, BLK), jnp.bfloat16)
+    plain[AT_ZERO] = jnp.zeros((TOK, BLK), jnp.bfloat16)
+    turned[AT_NONE] = jnp.zeros((BLK, TOK), jnp.bfloat16)
     sums[0] = jnp.zeros((BLK, BLK), jnp.float32)
 
     own_in.wait()
@@ -217,6 +217,7 @@
     for copy in meta_one:
         copy.start()
     right, left = push(0, 0, None, owner(1, 0)), push(0, 0, None, owner(3, 0))
+    opposite = push(0, 0, None, owner(2, 0))
     row_own = spread(0)
     to_sibling(0, 0)
     for copy in meta_one:
@@ -226,11 +227,9 @@
     for copy in meta_two:
         copy.start()
     right.wait_recv()
-    far_right = push(3, 0, 0, owner(1, 0))
     row_left = spread(3)
     to_sibling(3, 0)
     left.wait_recv()
-    far_left = push(1, 0, 1, owner(3, 0))
     row_right = spread(1)
     to_sibling(1, 0)
     for copy in meta_two:
@@ -257,8 +256,7 @@
         to_sibling(da, 2)
 
     pass_on(row_own, 0)
-    far_right.wait_recv()
-    far_left.wait_recv()
+    opposite.wait_recv()
     row_far = spread(2)
     to_sibling(2, 0)
     meta_three.wait_recv()
@@ -268,8 +266,10 @@
     x_in.wait()
     y_in.wait()
     for i in range(ND):
-        x[i] = x_flat[:, i * BLK : (i + 1) * BLK]
-        y[i] = y_flat[:, i * BLK : (i + 1) * BLK]
+        block = x_flat[:, i * BLK : (i + 1) * BLK]
+        plain[i] = block
+        turned[i] = block.T
+        plain[AT_Y + i] = y_flat[:, i * BLK : (i + 1) * BLK]
     pass_on(row_left, 3)
     pass_on(row_right, 1)
     finish()
@@ -293,16 +293,14 @@
     def products(step, carry):
         for inner in range(4):
             k = step * 4 + inner
-            gate = dot(x[at(ROW_CG, k)], weight(at(ROW_SG, k)), ((1,), (0,)))
-            up = dot(x[at(ROW_CU, k)], weight(at(ROW_SU, k)), ((1,), (0,)))
-            back = dot(y[at(ROW_CD, k)], weight(at(ROW_SD, k)), ((1,), (1,)))
+            gate = dot(plain[at(ROW_CG, k)], weight(at(ROW_SG, k)), ((1,), (0,)))
+            up = dot(plain[at(ROW_CU, k)], weight(at(ROW_SU, k)), ((1,), (0,)))
+            back = dot(plain[at(ROW_CD, k)], weight(at(ROW_SD, k)), ((1,), (1,)))
             sigmoid = jax.nn.sigmoid(gate)
             silu = gate * sigmoid
-            hid[k] = (silu * up).astype(jnp.bfloat16)
-            out_grad[k] = (back * up * sigmoid * (1.0 + gate * (1.0 - sigmoid))).astype(
-                jnp.bfloat16
-            )
-            out_grad[k + TRIPLES] = (back * silu).astype(jnp.bfloat16)
+            turned[AT_HID + k] = (silu * up).astype(jnp.bfloat16).T
+            plain[AT_GATE + k] = (back * up * sigmoid * (1.0 + gate * (1.0 - sigmoid))).astype(jnp.bfloat16)
+            plain[AT_UP + k] = (back * silu).astype(jnp.bfloat16)
         return carry
 
     lax.fori_loop(0, TRIPLES // 4, products, 0)
@@ -311,144 +309,93 @@
         made = []
         for inner in range(4):
             m = step * 4 + inner
-            made.append(
-                dot(
-                    out_grad[at(ROW_OUT, m)],
-                    weight(at(ROW_WGT, m)),
-                    ((1,), (1,)),
-                )
-            )
+            made.append(dot(plain[at(ROW_OUT, m)], weight(at(ROW_WGT, m)), ((1,), (1,))))
         for inner in range(4):
             m = step * 4 + inner
             run = made[inner] + sums[m] * keep[m, 0:1, :]
             sums[m + 1] = run
         return carry
 
-    lax.fori_loop(0, ENTRIES // 4, widths, 0)
-
     wide = D // ZSENDS
     z_sends = []
     for j in range(ZSENDS):
-        for i in range(j * ND // ZSENDS, (j + 1) * ND // ZSENDS):
-            passed[:, i * BLK : (i + 1) * BLK] = (
-                y[i].astype(jnp.float32) + sums[at(ROW_SUM, i)]
-            ).astype(jnp.bfloat16)
         here = pl.ds(j * wide, wide)
-        copy = remote(
-            passed.at[:, here], arriving.at[:, here], {"segment": lax.rem(z + layers - 1, layers)}
+        z_sends.append(
+            remote(passed.at[:, here], arriving.at[:, here], {"segment": lax.rem(z + layers - 1, layers)})
         )
-        z_sends.append(copy)
-
-        @pl.when(z > 0)
-        def _(copy=copy):
-            copy.start()
-
-    def slot_terms(step, carry):
-        for inner in range(2):
-            k = step * 2 + inner
-            made = (
-                dot(x[at(ROW_CG, k)], out_grad[k], ((0,), (0,))),
-                dot(x[at(ROW_CU, k)], out_grad[k + TRIPLES], ((0,), (0,))),
-                dot(hid[k], y[at(ROW_CD, k)], ((0,), (0,))),
-            )
-            for n in range(3):
-                terms[pl.ds(6 * k + 2 * n, 2)] = made[n].astype(jnp.bfloat16).reshape(2, GRAIN, BLK)
-        return carry
-
-    lax.fori_loop(0, TRIPLES // 2, slot_terms, 0)
-
-    group = 4 * PART
-
-    def term(device, g):
-        return terms[at(ROW_TERM, CAP * device + lax.div(g, 2)) + lax.rem(g, 2)]
-
-    def each(low, high, step):
-        def run(t, carry):
-            step(t)
-            return carry
-
-        lax.fori_loop(low, high, run, 0)
-
-    sib_copies = {}
-    for db in (2, 1, 3, 0):
-
-        def pack(t, db=db):
-            sib_out[db, t] = term(sib_owner(lax.div(t, PART), db), lax.rem(t, PART))
-
-        each(0, group, pack)
-        copy = remote(sib_out.at[db], sib_in.at[db], {"fsdp": sibling})
-        copy.start()
-        sends.append(copy)
-        sib_copies[db] = copy
-
-    def paired(db, t):
-        own = term(owner(lax.div(t, PART), db), lax.rem(t, PART))
-        return own.astype(jnp.float32) + sib_in[db, t].astype(jnp.float32)
-
-    def reduce_to(src, dst, target):
+
+    @pl.when(z > 0)
+    def _():
+        lax.fori_loop(0, ENTRIES // 4, widths, 0)
+        for j in range(ZSENDS):
+            for i in range(j * ND // ZSENDS, (j + 1) * ND // ZSENDS):
+                passed[:, i * BLK : (i + 1) * BLK] = (
+                    plain[AT_Y + i].astype(jnp.float32) + sums[at(ROW_SUM, i)]
+                ).astype(jnp.bfloat16)
+            z_sends[j].start()
+
+    def term(device, s):
+        n = CAP * device + s
+        return dot(turned[at(ROW_LEFT, n)], plain[at(ROW_RIGHT, n)], ((1,), (0,)))
+
+    def launch(src, dst, target):
         copy = remote(src, dst, {"fsdp": target})
         copy.start()
         sends.append(copy)
         return copy
 
-    sib_copies[2].wait_recv()
-
-    def pair_far(t):
-        pair_two[t] = paired(2, t).astype(jnp.bfloat16)
-
-    each(0, group, pair_far)
-    middle = group // 2
-    up_one = reduce_to(pair_two.at[0:middle], one_in.at[0:middle], owner(0, 1))
-    down_one = reduce_to(pair_two.at[middle:], one_in.at[middle:], owner(0, 3))
-    side_copies = []
-    for n, (db, came) in enumerate(((1, up_one), (3, down_one))):
-
-        def with_far(t, n=n, db=db):
-            pair_side[n, t] = (paired(db, t) + one_in[t].astype(jnp.float32)).astype(jnp.bfloat16)
-
-        def alone(t, n=n, db=db):
-            pair_side[n, t] = paired(db, t).astype(jnp.bfloat16)
-
-        sib_copies[db].wait_recv()
-        each(middle * (1 - n), middle * (2 - n), alone)
-        came.wait_recv()
-        each(middle * n, middle * (n + 1), with_far)
-        side_copies.append(reduce_to(pair_side.at[n], side_in.at[n], owner(0, db)))
-    sib_copies[0].wait_recv()
-    for copy in side_copies:
+    order = (2, 1, 3, 0)
+    sib_copies = {}
+    for da in order:
+
+        def fill(step, carry, da=da):
+            for inner in range(2):
+                db = 2 * step + inner
+                for s in range(CAP):
+                    sib_out[da, CAP * db + s] = term(sib_owner(da, db), s).astype(jnp.bfloat16)
+            return carry
+
+        lax.fori_loop(0, 2, fill, 0)
+        sib_copies[da] = launch(sib_out.at[da], sib_in.at[da], sibling)
+    side_copies = {}
+    for da in order:
+        sib_copies[da].wait_recv()
+
+        def pair(step, carry, da=da):
+            for inner in range(2):
+                db = 2 * step + inner
+                for s in range(CAP):
+                    i = CAP * db + s
+                    value = term(owner(da, db), s) + sib_in[da, i].astype(jnp.float32)
+                    pair_out[da, i] = value.astype(jnp.bfloat16)
+            return carry
+
+        lax.fori_loop(0, 2, pair, 0)
+        side_copies[da] = [
+            launch(pair_out.at[da, pl.ds(CAP * db, CAP)], side_in.at[da, pl.ds(CAP * (db - 1), CAP)], owner(0, db))
+            for db in (2, 1, 3)
+        ]
+
+    def ringed(da, s):
+        value = pair_out[da, s].astype(jnp.float32)
+        for n in range(3):
+            value = value + side_in[da, CAP * n + s].astype(jnp.float32)
+        return value
+
+    near_copies = []
+    for da in order[:3]:
+        for copy in side_copies[da]:
+            copy.wait_recv()
+        for s in range(CAP):
+            quad[da - 1, s] = ringed(da, s).astype(jnp.bfloat16)
+        near_copies.append(launch(quad.at[da - 1], near_in.at[da - 1], owner(da, 0)))
+    for copy in side_copies[0] + near_copies:
         copy.wait_recv()
-
-    def ringed(da, t):
-        i = PART * da + t
-        value = term(owner(da, 0), t).astype(jnp.float32) + sib_in[0, i].astype(jnp.float32)
-        return value + side_in[0, i].astype(jnp.float32) + side_in[1, i].astype(jnp.float32)
-
-    def opposite(t):
-        quad[2, t] = ringed(2, t).astype(jnp.bfloat16)
-
-    each(0, PART, opposite)
-    up_far = reduce_to(quad.at[2, 0:HALF], far_in.at[0:HALF], owner(1, 0))
-    down_far = reduce_to(quad.at[2, HALF:], far_in.at[HALF:], owner(3, 0))
-    near_copies = []
-    for n, (da, came) in enumerate(((1, up_far), (3, down_far))):
-
-        def with_opposite(t, da=da):
-            quad[da, t] = (ringed(da, t) + far_in[t].astype(jnp.float32)).astype(jnp.bfloat16)
-
-        def only(t, da=da):
-            quad[da, t] = ringed(da, t).astype(jnp.bfloat16)
-
-        each(HALF * (1 - n), HALF * (2 - n), only)
-        came.wait_recv()
-        each(HALF * n, HALF * (n + 1), with_opposite)
-        near_copies.append(reduce_to(quad.at[da], near_in.at[n], owner(da, 0)))
-    for copy in near_copies:
-        copy.wait_recv()
-
-    def final(t):
-        grads[t] = ringed(0, t) + near_in[0, t].astype(jnp.float32) + near_in[1, t].astype(jnp.float32)
-
-    each(0, PART, final)
+    for s in range(CAP):
+        value = ringed(0, s)
+        for n in range(3):
+            value = value + near_in[n, s].astype(jnp.float32)
+        grads[s] = value
 
     @pl.when(z == layers - 1)
     def _():
@@ -470,7 +417,7 @@
             copy.wait_send()
 
 
-COPIES = 7 + 4 + 16 + 16 + ZSENDS + 4 + 4 + 4
+COPIES = 7 + 3 + 16 + 16 + ZSENDS + 4 + 12 + 3
 
 
 def body(activations, output_grad, blocks, block_ids, owner_counts):
@@ -483,15 +430,15 @@
         kernel,
         out_shape=(
             jax.ShapeDtypeStruct((TOK, D), bf16),
-            jax.ShapeDtypeStruct((PART, GRAIN, BLK), f32),
+            jax.ShapeDtypeStruct((CAP, BLK, BLK), f32),
         ),
         in_specs=[smem, smem, hbm, hbm, hbm],
         out_specs=(free, vmem),
         scratch_shapes=[
             pltpu.VMEM((TOK, D), bf16),
             pltpu.VMEM((TOK, D), bf16),
-            pltpu.VMEM((ND, TOK, BLK), bf16),
-            pltpu.VMEM((ND, TOK, BLK), bf16),
+            pltpu.VMEM((AT_ZERO + 1, TOK, BLK), bf16),
+            pltpu.VMEM((AT_NONE + 1, BLK, TOK), bf16),
             pltpu.VMEM((2 * SLOTS + 2, GRAIN, BLK), bf16),
             pltpu.VMEM((4, 8, 128), jnp.int32),
             pltpu.VMEM((4, 8, 128), jnp.int32),
@@ -499,27 +446,21 @@
             pltpu.VMEM((16, 128), jnp.int32),
             pltpu.SMEM((16, 128), jnp.int32),
             pltpu.VMEM((ENTRIES, 8, 128), f32),
-            pltpu.VMEM((TRIPLES, TOK, BLK), bf16),
-            pltpu.VMEM((ENTRIES, TOK, BLK), bf16),
             pltpu.VMEM((ENTRIES + 1, TOK, BLK), f32),
             pltpu.VMEM((TOK, D), bf16),
             pltpu.VMEM((TOK, D), bf16),
-            pltpu.VMEM((6 * TRIPLES + 2, GRAIN, BLK), bf16),
-            pltpu.VMEM((4, 4 * PART, GRAIN, BLK), bf16),
-            pltpu.VMEM((4, 4 * PART, GRAIN, BLK), bf16),
-            pltpu.VMEM((4 * PART, GRAIN, BLK), bf16),
-            pltpu.VMEM((4 * PART, GRAIN, BLK), bf16),
-            pltpu.VMEM((2, 4 * PART, GRAIN, BLK), bf16),
-            pltpu.VMEM((2, 4 * PART, GRAIN, BLK), bf16),
-            pltpu.VMEM((4, PART, GRAIN, BLK), bf16),
-            pltpu.VMEM((PART, GRAIN, BLK), bf16),
-            pltpu.VMEM((2, PART, GRAIN, BLK), bf16),
+            pltpu.VMEM((4, 4 * CAP, BLK, BLK), bf16),
+            pltpu.VMEM((4, 4 * CAP, BLK, BLK), bf16),
+            pltpu.VMEM((4, 4 * CAP, BLK, BLK), bf16),
+            pltpu.VMEM((4, 3 * CAP, BLK, BLK), bf16),
+            pltpu.VMEM((3, CAP, BLK, BLK), bf16),
+            pltpu.VMEM((3, CAP, BLK, BLK), bf16),
             pltpu.SemaphoreType.DMA((5,)),
             pltpu.SemaphoreType.DMA((COPIES,)),
             pltpu.SemaphoreType.DMA((COPIES,)),
         ],
         compiler_params=pltpu.CompilerParams(
-            collective_id=0, has_side_effects=True, vmem_limit_bytes=48 * 1024 * 1024
+            collective_id=0, has_side_effects=True, vmem_limit_bytes=60 * 1024 * 1024
         ),
         name="relay",
     )(

time: 67.6 us -> 60 us (0.89)
  the two profiles are of different devices: /device:TPU:30 before, /device:TPU:225 now
where the time goes in v1:
time: 60 us; the launch traced here: 59.8 us
  Pallas kernels  55.5 us (92%)
  local copies, waits for them, and re-layouts  3.01 us (5%)
  between operations  1.29 us (2%)
    pallas_call x1, Pallas kernels, body(): pl.pallas_call(kernel, out_shape=(jax.ShapeDtypeStruct((TOK, D), bf16), j...  55.5 us
    unnamed x4, local copies, waits for them, and re-layouts  3.01 us

profile of v1, /device:TPU:225, one launch (start us, length us, event | category | flops | bytes accessed | tf_op | source)
XLA Modules:
  0.0 59.8 jit_solution(8349201412607806347)
XLA Ops:
  1.3 55.5 %relay.1 = (bf16[128,4096]{1,0:T(8,128)(2,1)}, f32[3,128,128]{2,1,0:T(8,128)}) custom-call(s32[1,3]{1,0:T(1,128)} %ids.1, s32[1,1]{1,0:T(1,128)S(6)} %copy.9.count, bf16[128,4096]{1,0:T(8,128)(2,1)} %bitcast.5, bf16[128,4096]{1,0:T(8,128)(2,1)} %bitcast.6, bf16[6,64,128]{2,1,0:T(8,128)(2,1)} %bitcast.9), custom_call_target="tpu_custom_call" | custom-call | tf_op jit(solution)/shard_map/relay/pallas_call | solution.py:429
  56.8 0.0 copy-start
  56.8 2.3 %copy.10 = bf16[1,128,4096]{2,1,0:T(8,128)(2,1)} copy(bf16[1,128,4096]{2,1,0:T(8,128)(2,1)} %bitcast.7) | data formatting | bytes 2097152
  59.1 0.0 copy-done
  59.1 0.7 %copy.11 = f32[1,3,128,128]{3,2,1,0:T(8,128)} copy(f32[1,3,128,128]{3,2,1,0:T(8,128)S(1)} %bitcast.8) | data formatting | bytes 393216
Async XLA Ops:
  56.8 2.3 %copy-start = (f32[3,128,128]{2,1,0:T(8,128)S(1)}, f32[3,128,128]{2,1,0:T(8,128)}, u32[]{:S(2)}) copy-start(f32[3,128,128]{2,1,0:T(8,128)} %get-tuple-element.5) | copy-start | bytes 589828

commit v2 on v1

--- a/solution.py
+++ b/solution.py
@@ -20,7 +20,9 @@
 TOK = 128
 TRIPLES = 20
 ENTRIES = 2 * TRIPLES
-ZSENDS = 8
+CHUNK = 64
+CUTS = 4
+ZSENDS = CUTS * (TOK // CHUNK)
 MESH = pl.DeviceIdType.MESH
 
 ROW_SG, ROW_SU, ROW_SD, ROW_CG, ROW_CU, ROW_CD = range(6)
@@ -108,6 +110,7 @@
     table,
     tbl,
     keep,
+    hid,
     sums,
     passed,
     zeros,
@@ -257,7 +260,7 @@
 
     pass_on(row_own, 0)
     opposite.wait_recv()
-    row_far = spread(2)
+    row_far = spread(2) + (push(2, 0, None, owner(0, 2)),)
     to_sibling(2, 0)
     meta_three.wait_recv()
     write_tables(meta_c[0] + meta_c[1], table, keep)
@@ -273,10 +276,14 @@
     pass_on(row_left, 3)
     pass_on(row_right, 1)
     finish()
-    pass_on(row_far, 2)
+    row_far[0].wait_recv()
+    to_sibling(2, 3)
+    row_far[1].wait_recv()
+    to_sibling(2, 1)
     finish()
     finish()
-    finish()
+    row_far[2].wait_recv()
+    to_sibling(2, 2)
     to_scalar.wait()
     for copy in to_sib:
         copy.wait_recv()
@@ -290,49 +297,68 @@
     def dot(left_side, right_side, dims):
         return lax.dot_general(left_side, right_side, (dims, ((), ())), preferred_element_type=jnp.float32)
 
-    def products(step, carry):
-        for inner in range(4):
-            k = step * 4 + inner
-            gate = dot(plain[at(ROW_CG, k)], weight(at(ROW_SG, k)), ((1,), (0,)))
-            up = dot(plain[at(ROW_CU, k)], weight(at(ROW_SU, k)), ((1,), (0,)))
-            back = dot(plain[at(ROW_CD, k)], weight(at(ROW_SD, k)), ((1,), (1,)))
-            sigmoid = jax.nn.sigmoid(gate)
-            silu = gate * sigmoid
-            turned[AT_HID + k] = (silu * up).astype(jnp.bfloat16).T
-            plain[AT_GATE + k] = (back * up * sigmoid * (1.0 + gate * (1.0 - sigmoid))).astype(jnp.bfloat16)
-            plain[AT_UP + k] = (back * silu).astype(jnp.bfloat16)
-        return carry
-
-    lax.fori_loop(0, TRIPLES // 4, products, 0)
-
-    def widths(step, carry):
-        made = []
-        for inner in range(4):
-            m = step * 4 + inner
-            made.append(dot(plain[at(ROW_OUT, m)], weight(at(ROW_WGT, m)), ((1,), (1,))))
-        for inner in range(4):
-            m = step * 4 + inner
-            run = made[inner] + sums[m] * keep[m, 0:1, :]
-            sums[m + 1] = run
-        return carry
-
-    wide = D // ZSENDS
+    def products(rows):
+        def step(i, carry):
+            for inner in range(4):
+                k = 4 * i + inner
+                gate = dot(plain[at(ROW_CG, k), rows], weight(at(ROW_SG, k)), ((1,), (0,)))
+                up = dot(plain[at(ROW_CU, k), rows], weight(at(ROW_SU, k)), ((1,), (0,)))
+                back = dot(plain[at(ROW_CD, k), rows], weight(at(ROW_SD, k)), ((1,), (1,)))
+                sigmoid = jax.nn.sigmoid(gate)
+                silu = gate * sigmoid
+                hid[k, rows] = (silu * up).astype(jnp.bfloat16)
+                plain[AT_GATE + k, rows] = (back * up * sigmoid * (1.0 + gate * (1.0 - sigmoid))).astype(
+                    jnp.bfloat16
+                )
+                plain[AT_UP + k, rows] = (back * silu).astype(jnp.bfloat16)
+            return carry
+
+        lax.fori_loop(0, TRIPLES // 4, step, 0)
+
+    def widths(rows):
+        def step(i, carry):
+            made = []
+            for inner in range(8):
+                m = 8 * i + inner
+                made.append(dot(plain[at(ROW_OUT, m), rows], weight(at(ROW_WGT, m)), ((1,), (1,))))
+            for inner in range(8):
+                m = 8 * i + inner
+                sums[m + 1, rows] = made[inner] + sums[m, rows] * keep[m, 0:1, :]
+            return carry
+
+        lax.fori_loop(0, ENTRIES // 8, step, 0)
+
     z_sends = []
-    for j in range(ZSENDS):
-        here = pl.ds(j * wide, wide)
+    for n in range(ZSENDS):
+        here = (pl.ds(n // CUTS * CHUNK, CHUNK), pl.ds(n % CUTS * (D // CUTS), D // CUTS))
         z_sends.append(
-            remote(passed.at[:, here], arriving.at[:, here], {"segment": lax.rem(z + layers - 1, layers)})
+            remote(passed.at[here], arriving.at[here], {"segment": lax.rem(z + layers - 1, layers)})
         )
 
     @pl.when(z > 0)
     def _():
-        lax.fori_loop(0, ENTRIES // 4, widths, 0)
-        for j in range(ZSENDS):
-            for i in range(j * ND // ZSENDS, (j + 1) * ND // ZSENDS):
-                passed[:, i * BLK : (i + 1) * BLK] = (
-                    plain[AT_Y + i].astype(jnp.float32) + sums[at(ROW_SUM, i)]
+        for n in range(ZSENDS):
+            rows = pl.ds(n // CUTS * CHUNK, CHUNK)
+            if n % CUTS == 0:
+                products(rows)
+                widths(rows)
+            for i in range(n % CUTS * ND // CUTS, (n % CUTS + 1) * ND // CUTS):
+                passed[rows, i * BLK : (i + 1) * BLK] = (
+                    plain[AT_Y + i, rows].astype(jnp.float32) + sums[at(ROW_SUM, i), rows]
                 ).astype(jnp.bfloat16)
-            z_sends[j].start()
+            z_sends[n].start()
+
+    @pl.when(z == 0)
+    def _():
+        products(pl.ds(0, TOK))
+
+    def turn(i, carry):
+        for inner in range(4):
+            k = 4 * i + inner
+            turned[AT_HID + k] = hid[k].T
+        return carry
+
+    lax.fori_loop(0, TRIPLES // 4, turn, 0)
 
     def term(device, s):
         n = CAP * device + s
@@ -345,36 +371,44 @@
         return copy
 
     order = (2, 1, 3, 0)
-    sib_copies = {}
-    for da in order:
-
-        def fill(step, carry, da=da):
+    sib_copies, side_copies = {}, {}
+
+    def fill(da):
+        def step(i, carry):
             for inner in range(2):
-                db = 2 * step + inner
+                db = 2 * i + inner
                 for s in range(CAP):
                     sib_out[da, CAP * db + s] = term(sib_owner(da, db), s).astype(jnp.bfloat16)
             return carry
 
-        lax.fori_loop(0, 2, fill, 0)
+        lax.fori_loop(0, 2, step, 0)
         sib_copies[da] = launch(sib_out.at[da], sib_in.at[da], sibling)
-    side_copies = {}
-    for da in order:
+
+    def pair(da):
+        def step(i, carry):
+            for inner in range(2):
+                db = 2 * i + inner
+                for s in range(CAP):
+                    n = CAP * db + s
+                    value = term(owner(da, db), s) + sib_in[da, n].astype(jnp.float32)
+                    pair_out[da, n] = value.astype(jnp.bfloat16)
+            return carry
+
         sib_copies[da].wait_recv()
-
-        def pair(step, carry, da=da):
-            for inner in range(2):
-                db = 2 * step + inner
-                for s in range(CAP):
-                    i = CAP * db + s
-                    value = term(owner(da, db), s) + sib_in[da, i].astype(jnp.float32)
-                    pair_out[da, i] = value.astype(jnp.bfloat16)
-            return carry
-
-        lax.fori_loop(0, 2, pair, 0)
+        lax.fori_loop(0, 2, step, 0)
         side_copies[da] = [
             launch(pair_out.at[da, pl.ds(CAP * db, CAP)], side_in.at[da, pl.ds(CAP * (db - 1), CAP)], owner(0, db))
             for db in (2, 1, 3)
         ]
+
+    fill(2)
+    fill(1)
+    fill(3)
+    pair(2)
+    fill(0)
+    pair(1)
+    pair(3)
+    pair(0)
 
     def ringed(da, s):
         value = pair_out[da, s].astype(jnp.float32)
@@ -446,6 +480,7 @@
             pltpu.VMEM((16, 128), jnp.int32),
             pltpu.SMEM((16, 128), jnp.int32),
             pltpu.VMEM((ENTRIES, 8, 128), f32),
+            pltpu.VMEM((TRIPLES, TOK, BLK), bf16),
             pltpu.VMEM((ENTRIES + 1, TOK, BLK), f32),
             pltpu.VMEM((TOK, D), bf16),
             pltpu.VMEM((TOK, D), bf16),

time: 60 us -> 58 us (0.967)
  Pallas kernels: 55.5 us -> 53.5 us
    pallas_call x1, Pallas kernels: 55.5 us -> 53.5 us  [body(): pl.pallas_call(kernel, out_shape=(jax.ShapeDtypeStruct((TOK, D), bf16), j...]
where the time goes in v2:
time: 58 us; the launch traced here: 57.8 us
  Pallas kernels  53.5 us (92%)
  local copies, waits for them, and re-layouts  3.01 us (5%)
  between operations  1.29 us (2%)
    pallas_call x1, Pallas kernels, body(): pl.pallas_call(kernel, out_shape=(jax.ShapeDtypeStruct((TOK, D), bf16), j...  53.5 us
    unnamed x4, local copies, waits for them, and re-layouts  3.01 us

profile of v2, /device:TPU:225, one launch (start us, length us, event | category | flops | bytes accessed | tf_op | source)
XLA Modules:
  0.0 57.8 jit_solution(6212954174177115203)
XLA Ops:
  1.3 53.5 %relay.1 = (bf16[128,4096]{1,0:T(8,128)(2,1)}, f32[3,128,128]{2,1,0:T(8,128)}) custom-call(s32[1,3]{1,0:T(1,128)} %ids.1, s32[1,1]{1,0:T(1,128)S(6)} %copy.9.count, bf16[128,4096]{1,0:T(8,128)(2,1)} %bitcast.5, bf16[128,4096]{1,0:T(8,128)(2,1)} %bitcast.6, bf16[6,64,128]{2,1,0:T(8,128)(2,1)} %bitcast.9), custom_call_target="tpu_custom_call" | custom-call | tf_op jit(solution)/shard_map/relay/pallas_call | solution.py:463
  54.8 0.0 copy-start
  54.8 2.3 %copy.10 = bf16[1,128,4096]{2,1,0:T(8,128)(2,1)} copy(bf16[1,128,4096]{2,1,0:T(8,128)(2,1)} %bitcast.7) | data formatting | bytes 2097152
  57.1 0.0 copy-done
  57.1 0.7 %copy.11 = f32[1,3,128,128]{3,2,1,0:T(8,128)} copy(f32[1,3,128,128]{3,2,1,0:T(8,128)S(1)} %bitcast.8) | data formatting | bytes 393216
Async XLA Ops:
  54.8 2.3 %copy-start = (f32[3,128,128]{2,1,0:T(8,128)S(1)}, f32[3,128,128]{2,1,0:T(8,128)}, u32[]{:S(2)}) copy-start(f32[3,128,128]{2,1,0:T(8,128)} %get-tuple-element.5) | copy-start | bytes 589828

commit v3 on v2

--- a/solution.py
+++ b/solution.py
@@ -120,6 +120,7 @@
     side_in,
     quad,
     near_in,
+    total,
     local_sem,
     send_sem,
     recv_sem,
@@ -186,6 +187,13 @@
     plain[AT_ZERO] = jnp.zeros((TOK, BLK), jnp.bfloat16)
     turned[AT_NONE] = jnp.zeros((BLK, TOK), jnp.bfloat16)
     sums[0] = jnp.zeros((BLK, BLK), jnp.float32)
+
+    blank = pltpu.make_async_copy(zeros, arriving, local_sem.at[4])
+
+    @pl.when(z == layers - 1)
+    def _():
+        zeros[...] = jnp.zeros(zeros.shape, jnp.bfloat16)
+        blank.start()
 
     own_in.wait()
     pl.semaphore_wait(barrier, len(partners))
@@ -429,17 +437,18 @@
         value = ringed(0, s)
         for n in range(3):
             value = value + near_in[n, s].astype(jnp.float32)
-        grads[s] = value
+        total[s] = value
+    grads_out = pltpu.make_async_copy(total, grads, local_sem.at[5])
+    grads_out.start()
+
+    for copy in meta_one + meta_two + [meta_three] + sends:
+        copy.wait_send()
+    grads_out.wait()
 
     @pl.when(z == layers - 1)
     def _():
-        zeros[...] = jnp.zeros(zeros.shape, jnp.bfloat16)
-        fill = pltpu.make_async_copy(zeros, arriving, local_sem.at[4])
-        fill.start()
-        fill.wait()
-
-    for copy in meta_one + meta_two + [meta_three] + sends:
-        copy.wait_send()
+        blank.wait()
+
     for copy in z_sends:
 
         @pl.when(z < layers - 1)
@@ -459,7 +468,6 @@
     hbm = pl.BlockSpec(memory_space=pltpu.HBM)
     free = pl.BlockSpec(memory_space=pl.ANY)
     smem = pl.BlockSpec(memory_space=pltpu.SMEM)
-    vmem = pl.BlockSpec(memory_space=pltpu.VMEM)
     arriving, grads = pl.pallas_call(
         kernel,
         out_shape=(
@@ -467,7 +475,7 @@
             jax.ShapeDtypeStruct((CAP, BLK, BLK), f32),
         ),
         in_specs=[smem, smem, hbm, hbm, hbm],
-        out_specs=(free, vmem),
+        out_specs=(free, free),
         scratch_shapes=[
             pltpu.VMEM((TOK, D), bf16),
             pltpu.VMEM((TOK, D), bf16),
@@ -490,7 +498,8 @@
             pltpu.VMEM((4, 3 * CAP, BLK, BLK), bf16),
             pltpu.VMEM((3, CAP, BLK, BLK), bf16),
             pltpu.VMEM((3, CAP, BLK, BLK), bf16),
-            pltpu.SemaphoreType.DMA((5,)),
+            pltpu.VMEM((CAP, BLK, BLK), f32),
+            pltpu.SemaphoreType.DMA((6,)),
             pltpu.SemaphoreType.DMA((COPIES,)),
             pltpu.SemaphoreType.DMA((COPIES,)),
         ],

time: 58 us -> 57.3 us (0.988)
  Pallas kernels: 53.5 us -> 52.8 us
    pallas_call x1, Pallas kernels: 53.5 us -> 52.8 us  [body(): pl.pallas_call(kernel, out_shape=(jax.ShapeDtypeStruct((TOK, D), bf16), j...]
where the time goes in v3:
time: 57.3 us; the launch traced here: 57.1 us
  Pallas kernels  52.8 us (92%)
  local copies, waits for them, and re-layouts  3.01 us (5%)
  between operations  1.29 us (2%)
    pallas_call x1, Pallas kernels, body(): pl.pallas_call(kernel, out_shape=(jax.ShapeDtypeStruct((TOK, D), bf16), j...  52.8 us
    unnamed x4, local copies, waits for them, and re-layouts  3.01 us

profile of v3, /device:TPU:225, one launch (start us, length us, event | category | flops | bytes accessed | tf_op | source)
XLA Modules:
  0.0 57.1 jit_solution(6483377164963907994)
XLA Ops:
  1.3 52.8 %relay.1 = (bf16[128,4096]{1,0:T(8,128)(2,1)}, f32[3,128,128]{2,1,0:T(8,128)}) custom-call(s32[1,3]{1,0:T(1,128)} %ids.1, s32[1,1]{1,0:T(1,128)S(6)} %copy.9.count, bf16[128,4096]{1,0:T(8,128)(2,1)} %bitcast.5, bf16[128,4096]{1,0:T(8,128)(2,1)} %bitcast.6, bf16[6,64,128]{2,1,0:T(8,128)(2,1)} %bitcast.9), custom_call_target="tpu_custom_call" | custom-call | tf_op jit(solution)/shard_map/relay/pallas_call | solution.py:471
  54.1 0.0 copy-start
  54.1 2.3 %copy.10 = bf16[1,128,4096]{2,1,0:T(8,128)(2,1)} copy(bf16[1,128,4096]{2,1,0:T(8,128)(2,1)} %bitcast.7) | data formatting | bytes 2097152
  56.4 0.0 copy-done
  56.4 0.7 %copy.11 = f32[1,3,128,128]{3,2,1,0:T(8,128)} copy(f32[1,3,128,128]{3,2,1,0:T(8,128)S(1)} %bitcast.8) | data formatting | bytes 393216
Async XLA Ops:
  54.1 2.3 %copy-start = (f32[3,128,128]{2,1,0:T(8,128)S(1)}, f32[3,128,128]{2,1,0:T(8,128)}, u32[]{:S(2)}) copy-start(f32[3,128,128]{2,1,0:T(8,128)} %get-tuple-element.5) | copy-start | bytes 589828

commit v4 on v3

--- a/solution.py
+++ b/solution.py
@@ -21,7 +21,7 @@
 TRIPLES = 20
 ENTRIES = 2 * TRIPLES
 CHUNK = 64
-CUTS = 4
+CUTS = 8
 ZSENDS = CUTS * (TOK // CHUNK)
 MESH = pl.DeviceIdType.MESH
 
@@ -268,7 +268,8 @@
 
     pass_on(row_own, 0)
     opposite.wait_recv()
-    row_far = spread(2) + (push(2, 0, None, owner(0, 2)),)
+    far = push(2, 0, None, owner(0, 2))
+    row_far = spread(2) + (far,)
     to_sibling(2, 0)
     meta_three.wait_recv()
     write_tables(meta_c[0] + meta_c[1], table, keep)
@@ -326,15 +327,15 @@
     def widths(rows):
         def step(i, carry):
             made = []
-            for inner in range(8):
-                m = 8 * i + inner
+            for inner in range(20):
+                m = 20 * i + inner
                 made.append(dot(plain[at(ROW_OUT, m), rows], weight(at(ROW_WGT, m)), ((1,), (1,))))
-            for inner in range(8):
-                m = 8 * i + inner
+            for inner in range(20):
+                m = 20 * i + inner
                 sums[m + 1, rows] = made[inner] + sums[m, rows] * keep[m, 0:1, :]
             return carry
 
-        lax.fori_loop(0, ENTRIES // 8, step, 0)
+        lax.fori_loop(0, ENTRIES // 20, step, 0)
 
     z_sends = []
     for n in range(ZSENDS):

time: 57.3 us -> 57.1 us (level)
  no operation moved by 1% of the time
where the time goes in v4:
time: 57.1 us; the launch traced here: 56.9 us
  Pallas kernels  52.6 us (92%)
  local copies, waits for them, and re-layouts  3.01 us (5%)
  between operations  1.29 us (2%)
    pallas_call x1, Pallas kernels, body(): pl.pallas_call(kernel, out_shape=(jax.ShapeDtypeStruct((TOK, D), bf16), j...  52.6 us
    unnamed x4, local copies, waits for them, and re-layouts  3.01 us

profile of v4, /device:TPU:225, one launch (start us, length us, event | category | flops | bytes accessed | tf_op | source)
XLA Modules:
  0.0 56.9 jit_solution(10695307693102871747)
XLA Ops:
  1.3 52.6 %relay.1 = (bf16[128,4096]{1,0:T(8,128)(2,1)}, f32[3,128,128]{2,1,0:T(8,128)}) custom-call(s32[1,3]{1,0:T(1,128)} %ids.1, s32[1,1]{1,0:T(1,128)S(6)} %copy.9.count, bf16[128,4096]{1,0:T(8,128)(2,1)} %bitcast.5, bf16[128,4096]{1,0:T(8,128)(2,1)} %bitcast.6, bf16[6,64,128]{2,1,0:T(8,128)(2,1)} %bitcast.9), custom_call_target="tpu_custom_call" | custom-call | tf_op jit(solution)/shard_map/relay/pallas_call | solution.py:472
  53.9 0.0 copy-start
  53.9 2.3 %copy.10 = bf16[1,128,4096]{2,1,0:T(8,128)(2,1)} copy(bf16[1,128,4096]{2,1,0:T(8,128)(2,1)} %bitcast.7) | data formatting | bytes 2097152
  56.2 0.0 copy-done
  56.2 0.7 %copy.11 = f32[1,3,128,128]{3,2,1,0:T(8,128)} copy(f32[1,3,128,128]{3,2,1,0:T(8,128)S(1)} %bitcast.8) | data formatting | bytes 393216
Async XLA Ops:
  53.9 2.3 %copy-start = (f32[3,128,128]{2,1,0:T(8,128)S(1)}, f32[3,128,128]{2,1,0:T(8,128)}, u32[]{:S(2)}) copy-start(f32[3,128,128]{2,1,0:T(8,128)} %get-tuple-element.5) | copy-start | bytes 589828
